TPU v7x, 512 devices: a whole 4x8x8 slice. The times are simulated.
512 devices in a mesh: serve: 32 (over z_hi, x, core), tensor: 16 (over z_lo, y).
Axes of the slice: x: 4, y: 8, z: 8 (z_hi: 4, z_lo: 2; z = z_hi * 2 + z_lo), core: 2. Of those that a mesh axis runs over, the one named last changes fastest.
Arguments:
- queries: bfloat16 [32768, 4096], P('serve', 'tensor'), may hold values from -8 to 8
- kv_cache: bfloat16 [32, 6400, 256], P('serve', 'tensor'), may hold values from -6 to 6
- question_slot: int32 [1024], P('serve'), may hold values from 0 to 3, as said below
- question_len: int32 [1024], P('serve'), may hold values from 1 to 32, 20480 in all
- out_weight: bfloat16 [4096, 8192], P(None, 'tensor'), may hold values from -0.375 to 0.375
Outputs:
- answers: bfloat16 [32768, 8192], P('serve', 'tensor')
Inputs may be any that keep to these rules, and one draw needn't show every extreme that they name: Question q of serving group g asks about the image held by serving group (g - question_slot[q]) mod 32; among one serving group's 32 questions every value 0 to 3 occurs exactly 32 / 4 times.
All inputs are finite; a program needn't handle non-finite values. No bound on the sum of `question_len` on one device may be relied on, other than what follows from the above.
Results may differ from a plain program's by a relative error of at most 0.0058.
Values may be sent and summed in bfloat16 or wider, within the bound.
A program may use at most 64 MiB of HBM per device.

v0:
```python
import jax
import jax.numpy as jnp
from jax import lax
from jax.sharding import PartitionSpec as P

KVH = 4
P_SIZE = 1600
QLEN = 32
NEED = 4


def swapped(shard, axis, bit):
    return lax.ppermute(shard, axis, [(i, i ^ 1 << bit) for i in range(lax.axis_size(axis))])


def shifted(value, axis, steps):
    count = lax.axis_size(axis)
    pairs = [(source, (source + steps) % count) for source in range(count)]
    return lax.ppermute(value, axis, pairs)


def attend(query_rows, key_value):
    row_count = query_rows.shape[0]
    head_count = key_value.shape[0]
    head_dim = key_value.shape[2] // 2
    grouped = query_rows.reshape(row_count, head_count, -1, head_dim)
    key_part = key_value[:, :, :head_dim]
    value_part = key_value[:, :, head_dim:]
    scores = jnp.einsum(
        "rkgd,kpd->kgrp", grouped, key_part, preferred_element_type=jnp.float32
    ) * head_dim ** (-0.5)
    row_max = jnp.max(scores, axis=3, keepdims=True)
    exp_scores = jnp.exp(scores - row_max)
    sum_exp = jnp.sum(exp_scores, axis=3, keepdims=True)
    weights = (exp_scores / sum_exp).astype(jnp.bfloat16)
    blended = jnp.einsum("kgrp,kpd->rkgd", weights, value_part, preferred_element_type=jnp.float32)
    return blended.reshape(row_count, -1)


def on_device(queries, kv_cache, question_slot, question_len, out_weight):
    row_count, col_count = queries.shape
    head_dim = kv_cache.shape[2] // 2
    question_count = row_count // QLEN
    per_slot = question_count // NEED
    head_piece = kv_cache[0]
    sharing = lax.axis_size("tensor") // KVH
    for bit_number in range(sharing.bit_length() - 1):
        partner_piece = swapped(head_piece, "tensor", bit_number)
        upper_member = lax.axis_index("tensor") // 2**bit_number % 2 == 1
        head_piece = jnp.where(
            upper_member,
            jnp.concatenate([partner_piece, head_piece], axis=0),
            jnp.concatenate([head_piece, partner_piece], axis=0),
        )
    key_value = head_piece.reshape(-1, P_SIZE, 2 * head_dim)
    ordering = jnp.argsort(question_slot, stable=True)
    inverse_order = jnp.argsort(ordering, stable=True)
    sorted_rows = queries.reshape(question_count, QLEN, col_count)[ordering]
    sorted_rows = sorted_rows.reshape(NEED, per_slot * QLEN, col_count)
    results = []
    for offset_back in range(NEED):
        if offset_back == 0:
            answer_part = attend(sorted_rows[0], key_value)
        else:
            visitors = shifted(sorted_rows[offset_back], "serve", -offset_back)
            answered = attend(visitors, key_value).astype(jnp.bfloat16)
            answer_part = shifted(answered, "serve", offset_back).astype(jnp.float32)
        results.append(answer_part)
    sorted_out = jnp.stack(results).reshape(question_count, QLEN, col_count)
    blended = sorted_out[inverse_order].reshape(row_count, col_count)
    token_pos = jnp.arange(row_count, dtype=jnp.int32) % QLEN
    live_rows = token_pos < jnp.repeat(question_len, QLEN, total_repeat_length=row_count)
    attended = jnp.where(live_rows[:, None], blended, 0.0).astype(jnp.bfloat16)
    zero_sum = jnp.zeros((row_count, out_weight.shape[1]), jnp.float32)
    gathered_cols = lax.all_gather(attended, "tensor", axis=1, tiled=True)
    weight_rows = lax.slice_in_dim(out_weight, 0, gathered_cols.shape[1], axis=0)
    answers = zero_sum + jnp.dot(gathered_cols, weight_rows, preferred_element_type=jnp.float32)
    return answers.astype(jnp.bfloat16)


def solution(mesh):
    return jax.shard_map(
        on_device,
        mesh=mesh,
        in_specs=(
            P("serve", "tensor"),
            P("serve", "tensor", None),
            P("serve"),
            P("serve"),
            P(None, "tensor"),
        ),
        out_specs=P("serve", "tensor"),
        check_vma=False,
    )
```

profile of v0, /device:TPU:48, one launch (start us, length us, event | category | flops | bytes accessed | tf_op | source)
XLA Modules:
  0.0 228.5 jit_solution(6938475126314562914)
XLA Ops:
  6.5 0.0 copy-start
  6.5 0.0 all-gather.2.cloned.1.call-start
  6.5 2.7 %collective-permute-start = (bf16[400,256]{1,0:T(8,128)(2,1)}, bf16[400,256]{1,0:T(8,128)(2,1)S(1)}, u32[]{:S(2)}, u32[]{:S(2)}) collective-permute-start(bf16[400,256]{1,0:T(8,128)(2,1)} %bitcast.204), channel_id=1, source_target_pairs={{0,1},{1,0},{2,3},{3,2},{4,5},{5,4},{6,7},{7,6},{8,9},{9,8},{10,11... | collective-permute-start | bytes 614408 | tf_op jit(solution)/shard_map/ppermute | solution.py:13
  9.3 2.3 sort.31
  11.5 0.0 copy-done
  11.5 0.6 gather_fusion
  12.2 13.1 %collective-permute-start.4 = (bf16[256,256]{1,0:T(8,128)(2,1)S(1)}, bf16[256,256]{1,0:T(8,128)(2,1)S(1)}, u32[]{:S(2)}, u32[]{:S(2)}) collective-permute-start(bf16[256,256]{1,0:T(8,128)(2,1)S(1)} %bitcast.212), channel_id=1, source_target_pairs={{0,480},{16,496},{32,0},{48,16},{64,32},{80,48},{96,64},{112,80},{... | collective-permute-start | bytes 393224 | tf_op jit(solution)/shard_map/ppermute | solution.py:19
  25.3 1.9 collective-permute-start.2
  27.2 2.8 %collective-permute-start.6 = (bf16[256,256]{1,0:T(8,128)(2,1)S(1)}, bf16[256,256]{1,0:T(8,128)(2,1)S(1)}, u32[]{:S(2)}, u32[]{:S(2)}) collective-permute-start(bf16[256,256]{1,0:T(8,128)(2,1)S(1)} %bitcast.210), channel_id=1, source_target_pairs={{0,464},{16,480},{32,496},{48,0},{64,16},{80,32},{96,48},{112,64},... | collective-permute-start | bytes 393224 | tf_op jit(solution)/shard_map/ppermute | solution.py:19
  30.1 1.8 fusion.33
  31.9 0.8 add_add_fusion.1
  32.7 4.4 %compare_select_fusion.1 = (s32[1024,1]{0,1:T(1,128)S(1)}, s32[1024,1]{0,1:T(1,128)S(1)}) fusion(s32[]{:T(128)} %bitcast.29, s32[]{:T(128)} %bitcast.30, s32[]{:T(128)} %bitcast.31, s32[]{:T(128)} %bitcast.32, s32[]{:T(128)} %bitcast.33, s32[]{:T(128)} %bitcast.35, s32[]{:T(128)} %bitcast.34, s32[1024,1]{0,1:T(1,128)S(1)} %bitcast.218, ...), kind=kLoop, calls=%fused_computation.75 | loop fusion | flops 14336 | bytes 16412 | tf_op jit(solution)/shard_map/jit(_take)/gather | solution.py:72
  37.1 2.1 fusion.32
  39.2 0.3 compare_reduce_fusion.24
  39.5 0.0 collective-permute-done
  39.5 1.2 maximum_select_fusion.1
  40.6 4.0 %collective-permute-start.1 = (bf16[800,256]{1,0:T(8,128)(2,1)S(1)}, bf16[800,256]{1,0:T(8,128)(2,1)S(1)}, u32[]{:S(2)}, u32[]{:S(2)}) collective-permute-start(bf16[800,256]{1,0:T(8,128)(2,1)S(1)} %maximum_select_fusion.1), channel_id=1, source_target_pairs={{0,2},{1,3},{2,0},{3,1},{4,6},{5,7},{6,4},{7,5},{8,10},{9,11},{10,... | collective-permute-start | bytes 1228808 | tf_op jit(solution)/shard_map/ppermute | solution.py:13
  44.7 16.3 %fusion.27 = pred[1024]{0:T(1024)(128)(4,1)S(1)} fusion(pred[1024]{0:T(1024)(128)(4,1)S(1)} %get-tuple-element.45, pred[1024]{0:T(1024)(128)(4,1)S(1)} %get-tuple-element.44, pred[1024]{0:T(1024)(128)(4,1)S(1)} %get-tuple-element.43, pred[1024]{0:T(1024)(128)(4,1)S(1)} %get-tuple-element.42, pred[1024]{0:T(1024)(128)(4,1)S(1)} %get-tuple-element.41, ...), kind=kLoop, calls=%fused_computation.85 | loop fusion | flops 41984 | bytes 34948 | tf_op jit(solution)/shard_map/lt | solution.py:72
  61.0 1.6 sort.32
  62.7 0.0 collective-permute-done.4
  62.7 0.1 copy.21
  62.8 0.0 collective-permute-done.2
  62.8 0.1 copy.18
  62.9 0.0 collective-permute-done.6
  62.9 0.1 copy.24
  63.0 0.0 collective-permute-done.1
  63.0 0.3 maximum_select_fusion
  63.4 0.6 bitcast_reduce_fusion
  64.0 0.4 fusion.7
  64.4 0.8 fusion.22
  65.2 0.1 copy.26
  65.3 2.5 %collective-permute-start.7 = (bf16[256,256]{1,0:T(8,128)(2,1)S(1)}, bf16[256,256]{1,0:T(8,128)(2,1)S(1)}, u32[]{:S(2)}, u32[]{:S(2)}) collective-permute-start(bf16[256,256]{1,0:T(8,128)(2,1)S(1)} %copy.26), channel_id=1, source_target_pairs={{0,48},{16,64},{32,80},{48,96},{64,112},{80,128},{96,144},{112,160... | collective-permute-start | bytes 393224 | tf_op jit(solution)/shard_map/ppermute | solution.py:19
  67.8 0.6 bitcast_reduce_fusion.2
  68.4 0.4 fusion.5
  68.8 0.8 fusion.16
  69.6 0.1 copy.20
  69.7 4.2 %collective-permute-start.3 = (bf16[256,256]{1,0:T(8,128)(2,1)S(1)}, bf16[256,256]{1,0:T(8,128)(2,1)S(1)}, u32[]{:S(2)}, u32[]{:S(2)}) collective-permute-start(bf16[256,256]{1,0:T(8,128)(2,1)S(1)} %copy.20), channel_id=1, source_target_pairs={{0,16},{16,32},{32,48},{48,64},{64,80},{80,96},{96,112},{112,128},... | collective-permute-start | bytes 393224 | tf_op jit(solution)/shard_map/ppermute | solution.py:19
  73.9 0.6 bitcast_reduce_fusion.1
  74.5 0.4 fusion.6
  74.9 0.8 fusion.19
  75.7 0.1 copy.23
  75.8 2.1 collective-permute-start.5
  78.0 0.6 bitcast_reduce_fusion.3
  78.6 0.4 fusion.4
  79.0 0.8 fusion.14
  79.8 0.1 copy.27
  79.9 0.0 collective-permute-done.7
  79.9 2.1 collective-permute-done.3
  82.0 8.1 %collective-permute-done.5 = bf16[256,256]{1,0:T(8,128)(2,1)S(1)} collective-permute-done((bf16[256,256]{1,0:T(8,128)(2,1)S(1)}, bf16[256,256]{1,0:T(8,128)(2,1)S(1)}, u32[]{:S(2)}, u32[]{:S(2)}) %collective-permute-start.5) | collective-permute-done | bytes 131104 | tf_op jit(solution)/shard_map/ppermute | solution.py:19
  90.2 0.1 pad_maximum_fusion
  90.3 0.6 gather_fusion.1
  90.8 1.0 fusion.25
  91.8 0.0 all-gather.2.cloned.1.call-update
  91.9 119.8 %all-gather.2.cloned.1.call-done = bf16[1024,4096]{1,0:T(8,128)(2,1)} async-done(((bf16[1024,256]{1,0:T(8,128)(2,1)}), bf16[1024,4096]{1,0:T(8,128)(2,1)}) %all-gather.2.cloned.1.call-update) | async-done | bytes 8388624 | tf_op jit(solution)/shard_map/all_gather | solution.py:75
  211.7 10.0 %convolution_convert_fusion = bf16[1024,512]{1,0:T(8,128)(2,1)} fusion(bf16[1024,4096]{1,0:T(8,128)(2,1)} %all-gather.2.cloned.1.call-done, bf16[4096,512]{1,0:T(8,128)(2,1)} %param.11), kind=kOutput, calls=%fused_computation.34 | convolution fusion | flops 4295491584 | bytes 13631488 | tf_op jit(solution)/shard_map/dot_general | solution.py:77
  (9 shorter events, 0.1 us)
Async XLA Ops:
  6.5 5.0 %copy-start = (bf16[1024,256]{1,0:T(8,128)(2,1)S(1)}, bf16[1024,256]{1,0:T(8,128)(2,1)}, u32[]{:S(2)}) copy-start(bf16[1024,256]{1,0:T(8,128)(2,1)} %param.7) | copy-start | bytes 1572868
  6.5 205.1 %all-gather.2.cloned.1.call-start = ((), (), s32[]{:S(2)}) async-start(), calls=%async_computation | async-start | bytes 8912896 | tf_op jit(solution)/shard_map/all_gather | solution.py:75
  6.5 32.9 %collective-permute-start = (bf16[400,256]{1,0:T(8,128)(2,1)}, bf16[400,256]{1,0:T(8,128)(2,1)S(1)}, u32[]{:S(2)}, u32[]{:S(2)}) collective-permute-start(bf16[400,256]{1,0:T(8,128)(2,1)} %bitcast.204), channel_id=1, source_target_pairs={{0,1},{1,0},{2,3},{3,2},{4,5},{5,4},{6,7},{7,6},{8,9},{9,8},{10,11... | collective-permute-start | bytes 614408 | tf_op jit(solution)/shard_map/ppermute | solution.py:13
  12.2 50.5 %collective-permute-start.4 = (bf16[256,256]{1,0:T(8,128)(2,1)S(1)}, bf16[256,256]{1,0:T(8,128)(2,1)S(1)}, u32[]{:S(2)}, u32[]{:S(2)}) collective-permute-start(bf16[256,256]{1,0:T(8,128)(2,1)S(1)} %bitcast.212), channel_id=1, source_target_pairs={{0,480},{16,496},{32,0},{48,16},{64,32},{80,48},{96,64},{112,80},{... | collective-permute-start | bytes 393224 | tf_op jit(solution)/shard_map/ppermute | solution.py:19
  25.3 37.5 %collective-permute-start.2 = (bf16[256,256]{1,0:T(8,128)(2,1)S(1)}, bf16[256,256]{1,0:T(8,128)(2,1)S(1)}, u32[]{:S(2)}, u32[]{:S(2)}) collective-permute-start(bf16[256,256]{1,0:T(8,128)(2,1)S(1)} %bitcast.211), channel_id=1, source_target_pairs={{0,496},{16,0},{32,16},{48,32},{64,48},{80,64},{96,80},{112,96},{1... | collective-permute-start | bytes 393224 | tf_op jit(solution)/shard_map/ppermute | solution.py:19
  27.2 35.7 %collective-permute-start.6 = (bf16[256,256]{1,0:T(8,128)(2,1)S(1)}, bf16[256,256]{1,0:T(8,128)(2,1)S(1)}, u32[]{:S(2)}, u32[]{:S(2)}) collective-permute-start(bf16[256,256]{1,0:T(8,128)(2,1)S(1)} %bitcast.210), channel_id=1, source_target_pairs={{0,464},{16,480},{32,496},{48,0},{64,16},{80,32},{96,48},{112,64},... | collective-permute-start | bytes 393224 | tf_op jit(solution)/shard_map/ppermute | solution.py:19
  40.6 22.4 %collective-permute-start.1 = (bf16[800,256]{1,0:T(8,128)(2,1)S(1)}, bf16[800,256]{1,0:T(8,128)(2,1)S(1)}, u32[]{:S(2)}, u32[]{:S(2)}) collective-permute-start(bf16[800,256]{1,0:T(8,128)(2,1)S(1)} %maximum_select_fusion.1), channel_id=1, source_target_pairs={{0,2},{1,3},{2,0},{3,1},{4,6},{5,7},{6,4},{7,5},{8,10},{9,11},{10,... | collective-permute-start | bytes 1228808 | tf_op jit(solution)/shard_map/ppermute | solution.py:13
  65.3 14.6 %collective-permute-start.7 = (bf16[256,256]{1,0:T(8,128)(2,1)S(1)}, bf16[256,256]{1,0:T(8,128)(2,1)S(1)}, u32[]{:S(2)}, u32[]{:S(2)}) collective-permute-start(bf16[256,256]{1,0:T(8,128)(2,1)S(1)} %copy.26), channel_id=1, source_target_pairs={{0,48},{16,64},{32,80},{48,96},{64,112},{80,128},{96,144},{112,160... | collective-permute-start | bytes 393224 | tf_op jit(solution)/shard_map/ppermute | solution.py:19
  69.7 12.3 %collective-permute-start.3 = (bf16[256,256]{1,0:T(8,128)(2,1)S(1)}, bf16[256,256]{1,0:T(8,128)(2,1)S(1)}, u32[]{:S(2)}, u32[]{:S(2)}) collective-permute-start(bf16[256,256]{1,0:T(8,128)(2,1)S(1)} %copy.20), channel_id=1, source_target_pairs={{0,16},{16,32},{32,48},{48,64},{64,80},{80,96},{96,112},{112,128},... | collective-permute-start | bytes 393224 | tf_op jit(solution)/shard_map/ppermute | solution.py:19
  75.8 14.3 %collective-permute-start.5 = (bf16[256,256]{1,0:T(8,128)(2,1)S(1)}, bf16[256,256]{1,0:T(8,128)(2,1)S(1)}, u32[]{:S(2)}, u32[]{:S(2)}) collective-permute-start(bf16[256,256]{1,0:T(8,128)(2,1)S(1)} %copy.23), channel_id=1, source_target_pairs={{0,32},{16,48},{32,64},{48,80},{64,96},{80,112},{96,128},{112,144}... | collective-permute-start | bytes 393224 | tf_op jit(solution)/shard_map/ppermute | solution.py:19
Sparse Core Ops, SparseCore 0:
  92.0 119.6 all-gather.1
where the time goes:
time: 229 us
  waiting for transfers between devices  130 us (57%)
  starting transfers between devices  33.4 us (15%)
  other arithmetic  30 us (13%)
  matrix products  15.5 us (7%)
  between operations  13.7 us (6%)
  local copies, waits for them, and re-layouts  5.85 us (3%)
    all_gather x1, waiting for transfers between devices, on_device(): gathered_cols = lax.all_gather(attended, 'tensor', axis=1, tiled=True)  120 us
    ppermute x6, starting transfers between devices, shifted(): return lax.ppermute(value, axis, pairs)  26.6 us
    lt x1, other arithmetic, on_device(): token_pos < jnp.repeat(question_len, QLEN, total_repeat_length=row_count)  16.3 us
    ppermute x6, waiting for transfers between devices, shifted(): return lax.ppermute(value, axis, pairs)  10.3 us
    dot_general x1, matrix products, on_device(): jnp.dot(gathered_cols, weight_rows, preferred_element_type=jnp.float32)  10 us
    ppermute x2, starting transfers between devices, swapped(): lax.ppermute(shard, axis, [(i, i ^ 1 << bit) for i in range(lax.axis_size...  6.75 us
    gather x2, other arithmetic, on_device(): jnp.repeat(question_len, QLEN, total_repeat_length=row_count)  4.66 us
  transfers between devices with their start and end apart: 9, of which 3 were waited for; matrix products, arithmetic and copies ran while one was open for 16% of the time, Pallas kernels for 0%

commit v1 on v0

v1 whole, which is shorter than its diff:
```python
import functools

import jax
import jax.numpy as jnp
from jax import lax
from jax.experimental import pallas as pl
from jax.experimental.pallas import tpu as pltpu
from jax.sharding import PartitionSpec as P

QLEN = 32
NEED = 4
RING = 8
SHARE = 4
HEAD_DIM = 128
SUBS = 2
MESH = pl.DeviceIdType.MESH
F32 = jnp.float32
BF16 = jnp.bfloat16


def event_order(chunks):
    events = [(3.5 * c + 3 * k, c, k) for c in range(chunks) for k in range(5)]
    return [(c, k) for _, c, k in sorted(events)]


def kernel(n_serve, q_hbm, kv_hbm, len_ref, w_hbm, out_hbm,
           sq, vq, ao, kvb, g, wo, wp, acc, ps, pr, ob,
           local_sem, ob_sem, kv_sr, kv_rr, kv_sl, kv_rl, q_s, q_r, ret_s, ret_r,
           w_s, w_r, wf_s, wf_r, ag_sr, ag_rr, ag_sl, ag_rl, p_s, p_r):
    s = lax.axis_index("serve")
    t = lax.axis_index("tensor")
    y = lax.rem(t, RING)
    z = t // RING
    p = lax.rem(t, SHARE)
    core = lax.rem(s, 2)
    right = (s, z * RING + lax.rem(y + 1, RING))
    left = (s, z * RING + lax.rem(y + RING - 1, RING))
    mate = (s, lax.rem(t + RING, 2 * RING))
    sibling = (s + 1 - 2 * core, t)
    owner = [None] + [(lax.rem(s + n_serve - j, n_serve), t) for j in range(1, NEED)]
    asker = [None] + [(lax.rem(s + j, n_serve), t) for j in range(1, NEED)]

    rows, cols = q_hbm.shape
    slot_rows = rows // NEED
    chunks = NEED * SUBS
    sub = slot_rows // SUBS
    piece = kv_hbm.shape[0]
    half = wo.shape[0]
    out_cols = wo.shape[1]
    wpart = half // 4
    scale = HEAD_DIM ** -0.5

    def remote(src, dst, send, recv, device):
        return pltpu.make_async_remote_copy(
            src_ref=src, dst_ref=dst, send_sem=send, recv_sem=recv,
            device_id=device, device_id_type=MESH)

    barrier = pltpu.get_barrier_semaphore()
    partners = [owner[3], asker[3], owner[2], asker[2], owner[1], asker[1], mate, right, left]
    for device in partners:
        pl.semaphore_signal(barrier, inc=1, device_id=device, device_id_type=MESH)

    q_load = pltpu.make_async_copy(q_hbm.at[pl.ds(0, slot_rows), :], sq, local_sem.at[0])
    q_load.start()

    def kv_rows(index):
        return kvb.at[pl.ds(pl.multiple_of(index * piece, 16), piece), :]

    kv_load = pltpu.make_async_copy(kv_hbm, kv_rows(p), local_sem.at[1])
    kv_load.start()
    w_load = pltpu.make_async_copy(
        w_hbm.at[pl.ds(pl.multiple_of(z * half, half), half), :], wo, local_sem.at[2])
    w_load.start()

    pl.semaphore_wait(barrier, len(partners))

    def kv_right(k):
        src = kv_hbm if k == 0 else kv_rows(p - k)
        return remote(src, kv_rows(p - k), kv_sr.at[k], kv_rr.at[k], right)

    def kv_left(k):
        src = kv_hbm if k == 0 else kv_rows(p + k)
        return remote(src, kv_rows(p + k), kv_sl.at[k], kv_rl.at[k], left)

    def kv_from_left(k):
        dst = kv_rows(p - k)
        return remote(dst, dst, kv_sr.at[k - 1], kv_rr.at[k - 1], left)

    def kv_from_right(k):
        dst = kv_rows(p + k)
        return remote(dst, dst, kv_sl.at[k - 1], kv_rl.at[k - 1], right)

    @pl.when(p < SHARE - 1)
    def _():
        kv_right(0).start()

    @pl.when(p > 0)
    def _():
        kv_left(0).start()

    def kv_step(k):
        @pl.when(p >= k)
        def _():
            kv_from_left(k).wait_recv()
            if k < SHARE - 1:
                @pl.when(p < SHARE - 1)
                def _():
                    kv_right(k).start()

        @pl.when(p + k < SHARE)
        def _():
            kv_from_right(k).wait_recv()
            if k < SHARE - 1:
                @pl.when(p > 0)
                def _():
                    kv_left(k).start()

    def ask(j, b):
        first = j * slot_rows + b * sub
        return remote(q_hbm.at[pl.ds(first, sub), :], vq.at[j - 1, pl.ds(b * sub, sub), :],
                      q_s.at[j - 1, b], q_r.at[j - 1, b], owner[j])

    for j in range(1, NEED):
        for b in range(SUBS):
            ask(j, b).start()

    def w_out(i):
        first = (1 - z) * half + core * (2 * wpart) + i * wpart
        return remote(w_hbm.at[pl.ds(pl.multiple_of(first, wpart), wpart), :],
                      wp.at[pl.ds(pl.multiple_of(core * (2 * wpart) + i * wpart, wpart), wpart), :],
                      w_s.at[i], w_r.at[i], mate)

    def w_swap(i):
        part = wp.at[pl.ds(pl.multiple_of(core * (2 * wpart) + i * wpart, wpart), wpart), :]
        return remote(part, part, wf_s.at[i], wf_r.at[i], sibling)

    def w_swapped(i):
        part = wp.at[pl.ds(pl.multiple_of((1 - core) * (2 * wpart) + i * wpart, wpart), wpart), :]
        return remote(part, part, wf_s.at[i], wf_r.at[i], sibling)

    for i in range(2):
        w_out(i).start()
    q_load.wait()
    kv_step(1)
    kv_step(2)
    kv_step(3)
    kv_load.wait()

    def attend(q_ref, o_ref):
        for h in range(cols // HEAD_DIM):
            query = q_ref[:, h * HEAD_DIM:(h + 1) * HEAD_DIM]
            scores = lax.dot_general(query, kvb[:, :HEAD_DIM], (((1,), (1,)), ((), ())),
                                     preferred_element_type=F32)
            top = jnp.max(scores, axis=1, keepdims=True)
            exps = jnp.exp((scores - top) * scale)
            total = jnp.sum(exps, axis=1, keepdims=True)
            blend = jnp.dot(exps.astype(BF16), kvb[:, HEAD_DIM:], preferred_element_type=F32)
            o_ref[:, h * HEAD_DIM:(h + 1) * HEAD_DIM] = (blend / total).astype(BF16)

    reach_right = [4 if c % 2 == 0 else 3 for c in range(chunks)]
    reach_left = [3 if c % 2 == 0 else 4 for c in range(chunks)]

    def block(origin, c):
        return g.at[lax.rem(origin + RING, RING), pl.ds(c * sub, sub), :]

    def go_right(c, k):
        part = block(y - k, c)
        return remote(part, part, ag_sr.at[c, k], ag_rr.at[c, k], right)

    def go_left(c, k):
        part = block(y + k, c)
        return remote(part, part, ag_sl.at[c, k], ag_rl.at[c, k], left)

    def from_left(c, k):
        part = block(y - k, c)
        return remote(part, part, ag_sr.at[c, k - 1], ag_rr.at[c, k - 1], left)

    def from_right(c, k):
        part = block(y + k, c)
        return remote(part, part, ag_sl.at[c, k - 1], ag_rl.at[c, k - 1], right)

    def answer(j, b):
        c = j * SUBS + b
        return remote(ao.at[j - 1, pl.ds(b * sub, sub), :], block(y, c),
                      ret_s.at[j - 1, b], ret_r.at[j - 1, b], asker[j])

    def answered(j, b):
        part = block(y, j * SUBS + b)
        return remote(part, part, ret_s.at[j - 1, b], ret_r.at[j - 1, b], owner[j])

    def visit(j, b):
        spot = pl.ds(b * sub, sub)
        remote(vq.at[j - 1, spot, :], vq.at[j - 1, spot, :],
               q_s.at[j - 1, b], q_r.at[j - 1, b], asker[j]).wait_recv()
        attend(vq.at[j - 1, spot, :], ao.at[j - 1, spot, :])
        answer(j, b).start()

    def partial(c):
        return remote(ps.at[c], pr.at[c], p_s.at[c], p_r.at[c], mate)

    def project(c):
        lhs = jnp.concatenate([g[i, c * sub:(c + 1) * sub, :] for i in range(RING)], axis=1)
        ps[c] = jnp.dot(lhs, wp[...], preferred_element_type=F32).astype(BF16)
        partial(c).start()
        acc[c * sub:(c + 1) * sub, :] = jnp.dot(lhs, wo[...], preferred_element_type=F32)

    def write(c):
        part = pl.ds(c * sub, sub)
        return pltpu.make_async_copy(ob.at[part, :], out_hbm.at[part, :], ob_sem.at[c])

    def finish(c):
        partial(c).wait_recv()
        token = lax.broadcasted_iota(jnp.int32, (QLEN, out_cols), 0)
        for i in range(sub // QLEN):
            part = slice(c * sub + i * QLEN, c * sub + (i + 1) * QLEN)
            total = acc[part, :] + pr[c, i * QLEN:(i + 1) * QLEN, :].astype(F32)
            live = token < len_ref[c * (sub // QLEN) + i]
            ob[part, :] = jnp.where(live, total, 0.0).astype(BF16)
        write(c).start()

    done = set()

    def event(c, k):
        if (c, k) in done:
            return
        done.add((c, k))
        if k == 0:
            if c < SUBS:
                attend(sq.at[pl.ds(c * sub, sub), :], g.at[y, pl.ds(c * sub, sub), :])
            else:
                answered(c // SUBS, c % SUBS).wait_recv()
            go_right(c, 0).start()
            go_left(c, 0).start()
            return
        if k <= reach_right[c]:
            from_left(c, k).wait_recv()
            if k < reach_right[c]:
                go_right(c, k).start()
        if k <= reach_left[c]:
            from_right(c, k).wait_recv()
            if k < reach_left[c]:
                go_left(c, k).start()
        if k == 4:
            if c == 0:
                w_load.wait()
                for i in range(2):
                    w_swapped(i).wait_recv()
            project(c)
            if c >= 1:
                finish(c - 1)

    def w_relay(i):
        w_out(i).wait_recv()
        w_swap(i).start()

    event(0, 0)
    event(1, 0)
    visit(1, 0)
    visit(1, 1)
    event(0, 1)
    event(1, 1)
    visit(2, 0)
    visit(2, 1)
    event(0, 2)
    event(1, 2)
    event(2, 0)
    visit(3, 0)
    event(3, 0)
    visit(3, 1)
    w_relay(0)
    event(0, 3)
    event(1, 3)
    event(2, 1)
    event(3, 1)
    w_relay(1)
    for c, k in event_order(chunks):
        event(c, k)
    finish(chunks - 1)

    for k in range(SHARE - 1):
        @pl.when(jnp.logical_and(p >= k, p < SHARE - 1))
        def _(k=k):
            kv_right(k).wait_send()

        @pl.when(jnp.logical_and(p + k < SHARE, p > 0))
        def _(k=k):
            kv_left(k).wait_send()
    for j in range(1, NEED):
        for b in range(SUBS):
            ask(j, b).wait_send()
            answer(j, b).wait_send()
    for i in range(2):
        w_out(i).wait_send()
        w_swap(i).wait_send()
    for c in range(chunks):
        for k in range(reach_right[c]):
            go_right(c, k).wait_send()
        for k in range(reach_left[c]):
            go_left(c, k).wait_send()
        partial(c).wait_send()
        write(c).wait()


def on_device(queries, kv_cache, question_slot, question_len, out_weight):
    rows, cols = queries.shape
    piece, width = kv_cache.shape[1:]
    depth, out_cols = out_weight.shape
    questions = rows // QLEN
    chunks = NEED * SUBS
    sub = rows // chunks
    slot_rows = rows // NEED
    dma = pltpu.SemaphoreType.DMA
    index = jnp.arange(questions, dtype=jnp.int32)
    same = question_slot[:, None] == question_slot[None, :]
    earlier = jnp.sum(jnp.where(same & (index[None, :] < index[:, None]), 1, 0), axis=1)
    pos = question_slot * (questions // NEED) + earlier
    chosen = pos[None, :] == index[:, None]
    order = jnp.sum(jnp.where(chosen, index[None, :], 0), axis=1)
    lengths = jnp.sum(jnp.where(chosen, question_len[None, :], 0), axis=1)
    sorted_rows = queries.reshape(questions, QLEN, cols)[order].reshape(rows, cols)
    ordered = pl.pallas_call(
        functools.partial(kernel, lax.axis_size("serve")),
        out_shape=jax.ShapeDtypeStruct((rows, out_cols), BF16),
        in_specs=[
            pl.BlockSpec(memory_space=pl.ANY),
            pl.BlockSpec(memory_space=pl.ANY),
            pl.BlockSpec(memory_space=pltpu.SMEM),
            pl.BlockSpec(memory_space=pl.ANY),
        ],
        out_specs=pl.BlockSpec(memory_space=pl.ANY),
        scratch_shapes=[
            pltpu.VMEM((slot_rows, cols), BF16),
            pltpu.VMEM((NEED - 1, slot_rows, cols), BF16),
            pltpu.VMEM((NEED - 1, slot_rows, cols), BF16),
            pltpu.VMEM((SHARE * piece, width), BF16),
            pltpu.VMEM((RING, rows, cols), BF16),
            pltpu.VMEM((depth // 2, out_cols), BF16),
            pltpu.VMEM((depth // 2, out_cols), BF16),
            pltpu.VMEM((rows, out_cols), F32),
            pltpu.VMEM((chunks, sub, out_cols), BF16),
            pltpu.VMEM((chunks, sub, out_cols), BF16),
            pltpu.VMEM((rows, out_cols), BF16),
            dma((3,)), dma((chunks,)),
            dma((3,)), dma((3,)), dma((3,)), dma((3,)),
            dma((NEED - 1, SUBS)), dma((NEED - 1, SUBS)), dma((NEED - 1, SUBS)), dma((NEED - 1, SUBS)),
            dma((2,)), dma((2,)), dma((2,)), dma((2,)),
            dma((chunks, 4)), dma((chunks, 4)), dma((chunks, 4)), dma((chunks, 4)),
            dma((chunks,)), dma((chunks,)),
        ],
        compiler_params=pltpu.CompilerParams(
            collective_id=0, has_side_effects=True, vmem_limit_bytes=56 * 1024 * 1024),
    )(sorted_rows, kv_cache.reshape(piece, width), lengths, out_weight)
    return ordered.reshape(questions, QLEN, out_cols)[pos].reshape(rows, out_cols)


def solution(mesh):
    return jax.shard_map(
        on_device,
        mesh=mesh,
        in_specs=(
            P("serve", "tensor"),
            P("serve", "tensor", None),
            P("serve"),
            P("serve"),
            P(None, "tensor"),
        ),
        out_specs=P("serve", "tensor"),
        check_vma=False,
    )
```

time: 229 us -> 104 us (0.45)
  the two profiles are of different devices: /device:TPU:48 before, /device:TPU:8 now
where the time goes in v1:
time: 104 us; the launch traced here: 103 us
  Pallas kernels  95.1 us (91%)
  local copies, waits for them, and re-layouts  5.22 us (5%)
  other arithmetic  2.95 us (3%)
    pallas_call x1, Pallas kernels, on_device(): pl.pallas_call(functools.partial(kernel, lax.axis_size('serve')), out_sha...  95.1 us
    gather x1, local copies, waits for them, and re-layouts, on_device(): ordered.reshape(questions, QLEN, out_cols)[pos].reshape(rows, out_cols)  2.81 us

profile of v1, /device:TPU:8, one launch (start us, length us, event | category | flops | bytes accessed | tf_op | source)
XLA Modules:
  0.0 103.3 jit_solution(802523358732804200)
XLA Ops:
  0.0 0.0 copy-start
  0.0 1.0 %copy-done = bf16[1024,256]{1,0:T(8,128)(2,1)S(1)} copy-done((bf16[1024,256]{1,0:T(8,128)(2,1)S(1)}, bf16[1024,256]{1,0:T(8,128)(2,1)}, u32[]{:S(2)}) %copy-start) | copy-done | bytes 524312
  1.0 0.9 select_reduce_fusion.2
  2.0 0.7 compare_select_fusion
  2.6 1.4 %select_reduce_fusion = (s32[32]{0:T(128)}, s32[32]{0:T(128)S(1)}) fusion(s32[32]{0:T(128)} %param.8, s32[32]{0:T(128)S(1)} %get-tuple-element.8), kind=kLoop, calls=%fused_computation.2 | loop fusion | flops 5056 | bytes 512 | tf_op jit(solution)/shard_map/reduce_sum | solution.py:319
  4.0 1.4 %gather_fusion = bf16[32,32,256]{2,1,0:T(8,128)(2,1)} fusion(bf16[32,32,256]{2,1,0:T(8,128)(2,1)S(1)} %bitcast.9, s32[1024]{0:T(1024)S(1)} %pad_clamp_fusion.1), kind=kCustom, calls=%fused_computation | custom fusion | bytes 1048704 | tf_op jit(solution)/shard_map/gather | solution.py:320
  5.4 95.1 %shard_map.55 = bf16[1024,512]{1,0:T(8,128)(2,1)} custom-call(bf16[1024,256]{1,0:T(8,128)(2,1)} %bitcast.11, bf16[400,256]{1,0:T(8,128)(2,1)} %bitcast.12, s32[32]{0:T(128)} %get-tuple-element.5.len_ref, bf16[4096,512]{1,0:T(8,128)(2,1)} %w_hbm.1), custom_call_target="tpu_custom_call" | custom-call | tf_op jit(solution)/shard_map/pallas_call | solution.py:321
  100.5 2.8 %gather_fusion.1 = bf16[32,32,512]{2,1,0:T(8,128)(2,1)} fusion(bf16[32,32,512]{2,1,0:T(8,128)(2,1)} %bitcast.10, s32[1024]{0:T(1024)S(1)} %pad_clamp_fusion), kind=kCustom, calls=%fused_computation.1 | custom fusion | bytes 2097280 | tf_op jit(solution)/shard_map/gather | solution.py:353
  (3 shorter events, 0.0 us)
Async XLA Ops:
  0.0 1.0 %copy-start = (bf16[1024,256]{1,0:T(8,128)(2,1)S(1)}, bf16[1024,256]{1,0:T(8,128)(2,1)}, u32[]{:S(2)}) copy-start(bf16[1024,256]{1,0:T(8,128)(2,1)} %param.5) | copy-start | bytes 1572868

commit v2 on v0

v2 whole, which is shorter than its diff:
```python
import functools

import jax
import jax.numpy as jnp
from jax import lax
from jax.experimental import pallas as pl
from jax.experimental.pallas import tpu as pltpu
from jax.sharding import PartitionSpec as P

QLEN = 32
NEED = 4
RING = 8
SHARE = 4
HEAD_DIM = 128
MESH = pl.DeviceIdType.MESH
F32 = jnp.float32
BF16 = jnp.bfloat16
VMEM_LIMIT = 56 * 1024 * 1024


def remote(src, dst, send, recv, device):
    return pltpu.make_async_remote_copy(
        src_ref=src, dst_ref=dst, send_sem=send, recv_sem=recv,
        device_id=device, device_id_type=MESH)


def greet(partners):
    barrier = pltpu.get_barrier_semaphore()
    for device in partners:
        pl.semaphore_signal(barrier, inc=1, device_id=device, device_id_type=MESH)
    return lambda: pl.semaphore_wait(barrier, len(partners))


def attend(q_ref, kvb, o_ref):
    for h in range(q_ref.shape[1] // HEAD_DIM):
        query = q_ref[:, h * HEAD_DIM:(h + 1) * HEAD_DIM]
        scores = lax.dot_general(query, kvb[:, :HEAD_DIM], (((1,), (1,)), ((), ())),
                                 preferred_element_type=F32)
        top = jnp.max(scores, axis=1, keepdims=True)
        exps = jnp.exp((scores - top) * HEAD_DIM ** -0.5)
        total = jnp.sum(exps, axis=1, keepdims=True)
        blend = jnp.dot(exps.astype(BF16), kvb[:, HEAD_DIM:], preferred_element_type=F32)
        o_ref[:, h * HEAD_DIM:(h + 1) * HEAD_DIM] = (blend / total).astype(BF16)


def chunk_list(rows):
    sub = rows // (2 * NEED)
    chunks = [(i * sub, sub, i // 2) for i in range(2 * NEED - 1)]
    return chunks + [(rows - sub, sub // 2, NEED - 1), (rows - sub // 2, sub // 2, NEED - 1)]


def exchange(n_serve, chunks, q_hbm, kv_hbm, slot_ref, len_ref, w_hbm, out_hbm, place_out,
             qv, sq, vq, ao, kvb, g, wo, wp, acc, ps, pr, ob, live_ref,
             local_sem, ob_sem, kv_sr, kv_rr, kv_sl, kv_rl, q_s, q_r, ret_s, ret_r,
             w_s, w_r, wf_s, wf_r, ag_sr, ag_rr, ag_sl, ag_rl, p_s, p_r):
    s = lax.axis_index("serve")
    t = lax.axis_index("tensor")
    y = lax.rem(t, RING)
    z = t // RING
    p = lax.rem(t, SHARE)
    core = lax.rem(s, 2)
    right = (s, z * RING + lax.rem(y + 1, RING))
    left = (s, z * RING + lax.rem(y + RING - 1, RING))
    mate = (s, lax.rem(t + RING, 2 * RING))
    sibling = (s + 1 - 2 * core, t)
    owner = [None] + [(lax.rem(s + n_serve - j, n_serve), t) for j in range(1, NEED)]
    asker = [None] + [(lax.rem(s + j, n_serve), t) for j in range(1, NEED)]
    rows, cols = q_hbm.shape
    questions = rows // QLEN
    slot_rows = rows // NEED
    piece = kv_hbm.shape[0]
    half, out_cols = wo.shape
    wpart = half // 4

    wait_entry = greet([owner[3], asker[3], owner[2], asker[2], owner[1], asker[1], mate, right, left])
    q_load = pltpu.make_async_copy(q_hbm, qv, local_sem.at[0])
    q_load.start()

    def kv_rows(index):
        return kvb.at[pl.ds(pl.multiple_of(index * piece, 16), piece), :]

    kv_load = pltpu.make_async_copy(kv_hbm, kv_rows(p), local_sem.at[1])
    kv_load.start()
    w_load = pltpu.make_async_copy(
        w_hbm.at[pl.ds(pl.multiple_of(z * half, half), half), :], wo, local_sem.at[2])
    w_load.start()
    wait_entry()

    def kv_right(k):
        src = kv_hbm if k == 0 else kv_rows(p - k)
        return remote(src, kv_rows(p - k), kv_sr.at[k], kv_rr.at[k], right)

    def kv_left(k):
        src = kv_hbm if k == 0 else kv_rows(p + k)
        return remote(src, kv_rows(p + k), kv_sl.at[k], kv_rl.at[k], left)

    @pl.when(p < SHARE - 1)
    def _():
        kv_right(0).start()

    @pl.when(p > 0)
    def _():
        kv_left(0).start()

    def kv_step(k):
        @pl.when(p >= k)
        def _():
            dst = kv_rows(p - k)
            remote(dst, dst, kv_sr.at[k - 1], kv_rr.at[k - 1], left).wait_recv()
            if k < SHARE - 1:
                @pl.when(p < SHARE - 1)
                def _():
                    kv_right(k).start()

        @pl.when(p + k < SHARE)
        def _():
            dst = kv_rows(p + k)
            remote(dst, dst, kv_sl.at[k - 1], kv_rl.at[k - 1], right).wait_recv()
            if k < SHARE - 1:
                @pl.when(p > 0)
                def _():
                    kv_left(k).start()

    slot = slot_ref[...]
    mine = (lax.broadcasted_iota(jnp.int32, (8, questions), 0) == slot).astype(F32)
    before = (lax.broadcasted_iota(jnp.int32, (questions, questions), 0)
              < lax.broadcasted_iota(jnp.int32, (questions, questions), 1)).astype(F32)
    rank = jnp.dot(mine.astype(BF16), before.astype(BF16), preferred_element_type=F32)
    place = jnp.sum(mine * rank, axis=0, keepdims=True) + slot.astype(F32) * (questions // NEED)
    spread = (lax.broadcasted_iota(jnp.int32, (questions, rows), 1) // QLEN
              == lax.broadcasted_iota(jnp.int32, (questions, rows), 0)).astype(BF16)
    both = jnp.concatenate([place, len_ref[...].astype(F32), jnp.zeros((6, questions), F32)], axis=0)
    both = jnp.dot(both.astype(BF16), spread, preferred_element_type=F32).astype(jnp.int32)
    token = lax.broadcasted_iota(jnp.int32, (1, rows), 1) % QLEN
    row = both[0:1, :] * QLEN + token
    live = (token < both[1:2, :]).astype(F32)
    place_out[...] = place.astype(jnp.int32)

    q_load.wait()

    def sort(j):
        first = j * slot_rows
        chosen = (lax.broadcasted_iota(jnp.int32, (slot_rows, rows), 0) + first == row).astype(F32)
        sq[pl.ds(first, slot_rows), :] = jnp.dot(
            chosen.astype(BF16), qv[...], preferred_element_type=F32).astype(BF16)
        live_ref[pl.ds(first, slot_rows), :] = jnp.sum(chosen * live, axis=1, keepdims=True)

    def spot(c):
        first, size, _ = chunks[c]
        return pl.ds(first - slot_rows, size)

    def part_of(ref, c):
        first, size, _ = chunks[c]
        return ref.at[pl.ds(first, size), :]

    def ask(c):
        return remote(part_of(sq, c), vq.at[spot(c), :], q_s.at[c], q_r.at[c], owner[chunks[c][2]])

    def w_part(side, i):
        return wp.at[pl.ds(pl.multiple_of(side * (2 * wpart) + i * wpart, wpart), wpart), :]

    def w_out(i):
        first = (1 - z) * half + core * (2 * wpart) + i * wpart
        return remote(w_hbm.at[pl.ds(pl.multiple_of(first, wpart), wpart), :], w_part(core, i),
                      w_s.at[i], w_r.at[i], mate)

    def w_swap(i):
        return remote(w_part(core, i), w_part(core, i), wf_s.at[i], wf_r.at[i], sibling)

    def w_relay(i):
        w_out(i).wait_recv()
        w_swap(i).start()

    def w_ready():
        w_load.wait()
        for i in range(2):
            part = w_part(1 - core, i)
            remote(part, part, wf_s.at[i], wf_r.at[i], sibling).wait_recv()

    count = len(chunks)
    visitors = [c for c in range(count) if chunks[c][2] > 0]
    for j in range(1, NEED):
        sort(j)
        for c in visitors:
            if chunks[c][2] == j:
                ask(c).start()
    w_out(0).start()
    w_out(1).start()
    kv_step(1)
    sort(0)
    kv_step(2)
    kv_step(3)
    kv_load.wait()

    reach_right = [4 if c % 2 == 0 else 3 for c in range(len(chunks))]
    reach_left = [3 if c % 2 == 0 else 4 for c in range(len(chunks))]

    def block(origin, c):
        first, size, _ = chunks[c]
        return g.at[lax.rem(origin + RING, RING), pl.ds(first, size), :]

    def go_right(c, k):
        return remote(block(y - k, c), block(y - k, c),
                      ag_sr.at[c, k], ag_rr.at[c, k], right)

    def go_left(c, k):
        return remote(block(y + k, c), block(y + k, c),
                      ag_sl.at[c, k], ag_rl.at[c, k], left)

    def from_left(c, k):
        part = block(y - k, c)
        return remote(part, part, ag_sr.at[c, k - 1], ag_rr.at[c, k - 1], left)

    def from_right(c, k):
        part = block(y + k, c)
        return remote(part, part, ag_sl.at[c, k - 1], ag_rl.at[c, k - 1], right)

    def answer(c):
        return remote(ao.at[spot(c), :], block(y, c), ret_s.at[c], ret_r.at[c], asker[chunks[c][2]])

    def visit(c):
        slot = chunks[c][2]
        remote(vq.at[spot(c), :], vq.at[spot(c), :], q_s.at[c], q_r.at[c], asker[slot]).wait_recv()
        attend(vq.at[spot(c), :], kvb, ao.at[spot(c), :])
        answer(c).start()

    def partial(c):
        return remote(part_of(ps, c), part_of(pr, c), p_s.at[c], p_r.at[c], mate)

    def project(c):
        first, size, slot = chunks[c]
        lhs = jnp.concatenate([g[i, first:first + size, :] for i in range(RING)], axis=1)
        ps[first:first + size, :] = jnp.dot(lhs, wp[...], preferred_element_type=F32).astype(BF16)
        partial(c).start()
        acc[first:first + size, :] = jnp.dot(lhs, wo[...], preferred_element_type=F32)

    def write(c):
        return pltpu.make_async_copy(part_of(ob, c), part_of(out_hbm, c), ob_sem.at[c])

    def finish(c):
        first, size, _ = chunks[c]
        partial(c).wait_recv()
        part = slice(first, first + size)
        total = acc[part, :] + pr[part, :].astype(F32)
        ob[part, :] = jnp.where(live_ref[part, :] > 0.5, total, 0.0).astype(BF16)
        write(c).start()

    def start(c):
        if chunks[c][2] > 0:
            part = block(y, c)
            remote(part, part, ret_s.at[c], ret_r.at[c], owner[chunks[c][2]]).wait_recv()
        else:
            attend(part_of(sq, c), kvb, block(y, c))
        go_right(c, 0).start()
        go_left(c, 0).start()

    def step(c, k):
        if k <= reach_right[c]:
            from_left(c, k).wait_recv()
            if k < reach_right[c]:
                go_right(c, k).start()
        if k <= reach_left[c]:
            from_right(c, k).wait_recv()
            if k < reach_left[c]:
                go_left(c, k).start()

    tasks = []
    ready = {}
    for c, (first, size, slot) in enumerate(chunks):
        begin = 3.5 * first
        if slot > 0:
            tasks.append((begin, functools.partial(start, c)))
        for k in range(1, 5):
            tasks.append((begin + LAG * k * max(size, 96), functools.partial(step, c, k)))
        ready[c] = max(begin + LAG * 4 * max(size, 96) + 1, W_TIME + 2 + c)
        tasks.append((ready[c], functools.partial(project, c)))
        tasks.append((ready[c] + 450 if c < count - 1 else 1e9, functools.partial(finish, c)))
    for i, c in enumerate(visitors):
        tasks.append((VISIT[chunks[c][2]] + i, functools.partial(visit, c)))
    tasks.append((15, functools.partial(w_relay, 0)))
    tasks.append((W_TIME, functools.partial(w_relay, 1)))
    tasks.append((W_TIME + 1, w_ready))
    tasks.sort(key=lambda task: task[0])
    start(0)
    start(1)
    for _, task in tasks:
        task()

    for k in range(SHARE - 1):
        @pl.when(jnp.logical_and(p >= k, p < SHARE - 1))
        def _(k=k):
            kv_right(k).wait_send()

        @pl.when(jnp.logical_and(p + k < SHARE, p > 0))
        def _(k=k):
            kv_left(k).wait_send()
    for c in visitors:
        ask(c).wait_send()
        answer(c).wait_send()
    for i in range(2):
        w_out(i).wait_send()
        w_swap(i).wait_send()
    for c in range(count):
        for k in range(reach_right[c]):
            go_right(c, k).wait_send()
        for k in range(reach_left[c]):
            go_left(c, k).wait_send()
        partial(c).wait_send()
        write(c).wait()


LAG = 2.2
W_TIME = 900
VISIT = [0, 10, 310, 620]


def unsort(place_ref, ordered, out, held, in_sem, out_sem):
    questions = place_ref.shape[0]

    def fetch(q):
        return pltpu.make_async_copy(
            ordered.at[pl.ds(pl.multiple_of(place_ref[q] * QLEN, QLEN), QLEN), :],
            held.at[pl.ds(q * QLEN, QLEN), :], in_sem.at[q])

    def store(q):
        part = pl.ds(q * QLEN, QLEN)
        return pltpu.make_async_copy(held.at[part, :], out.at[part, :], out_sem.at[q])

    for q in range(questions):
        fetch(q).start()
    for q in range(questions):
        fetch(q).wait()
        store(q).start()
    for q in range(questions):
        store(q).wait()


def on_device(queries, kv_cache, question_slot, question_len, out_weight):
    rows, cols = queries.shape
    piece, width = kv_cache.shape[1:]
    depth, out_cols = out_weight.shape
    questions = rows // QLEN
    slot_rows = rows // NEED
    half = depth // 2
    chunks = chunk_list(rows)
    count = len(chunks)
    dma = pltpu.SemaphoreType.DMA
    vmem, anywhere = pl.BlockSpec(memory_space=pltpu.VMEM), pl.BlockSpec(memory_space=pl.ANY)
    ordered, place = pl.pallas_call(
        functools.partial(exchange, lax.axis_size("serve"), chunks),
        out_shape=(
            jax.ShapeDtypeStruct((rows, out_cols), BF16),
            jax.ShapeDtypeStruct((1, questions), jnp.int32),
        ),
        in_specs=[anywhere, anywhere, vmem, vmem, anywhere],
        out_specs=(anywhere, vmem),
        scratch_shapes=[
            pltpu.VMEM((rows, cols), BF16),
            pltpu.VMEM((rows, cols), BF16),
            pltpu.VMEM((rows - slot_rows, cols), BF16),
            pltpu.VMEM((rows - slot_rows, cols), BF16),
            pltpu.VMEM((SHARE * piece, width), BF16),
            pltpu.VMEM((RING, rows, cols), BF16),
            pltpu.VMEM((half, out_cols), BF16),
            pltpu.VMEM((half, out_cols), BF16),
            pltpu.VMEM((rows, out_cols), F32),
            pltpu.VMEM((rows, out_cols), BF16),
            pltpu.VMEM((rows, out_cols), BF16),
            pltpu.VMEM((rows, out_cols), BF16),
            pltpu.VMEM((rows, 1), F32),
            dma((3,)), dma((count,)),
            dma((3,)), dma((3,)), dma((3,)), dma((3,)),
            dma((count,)), dma((count,)), dma((count,)), dma((count,)),
            dma((2,)), dma((2,)), dma((2,)), dma((2,)),
            dma((count, 4)), dma((count, 4)), dma((count, 4)), dma((count, 4)),
            dma((count,)), dma((count,)),
        ],
        compiler_params=pltpu.CompilerParams(
            collective_id=0, has_side_effects=True, vmem_limit_bytes=VMEM_LIMIT),
        name="exchange",
    )(queries, kv_cache.reshape(piece, width), question_slot.reshape(1, questions),
      question_len.reshape(1, questions), out_weight)
    return pl.pallas_call(
        unsort,
        out_shape=jax.ShapeDtypeStruct((rows, out_cols), BF16),
        in_specs=[pl.BlockSpec(memory_space=pltpu.SMEM), anywhere],
        out_specs=anywhere,
        scratch_shapes=[pltpu.VMEM((rows, out_cols), BF16), dma((questions,)), dma((questions,))],
        name="unsort",
    )(place.reshape(questions), ordered)


def solution(mesh):
    return jax.shard_map(
        on_device,
        mesh=mesh,
        in_specs=(
            P("serve", "tensor"),
            P("serve", "tensor", None),
            P("serve"),
            P("serve"),
            P(None, "tensor"),
        ),
        out_specs=P("serve", "tensor"),
        check_vma=False,
    )
```

time: 229 us -> 113 us (0.49)
  the two profiles are of different devices: /device:TPU:48 before, /device:TPU:64 now
where the time goes in v2:
time: 113 us
  Pallas kernels  113 us (100%)
    pallas_call x1, Pallas kernels, on_device(): pl.pallas_call(functools.partial(exchange, lax.axis_size('serve'), chunks...  109 us
    pallas_call x1, Pallas kernels, on_device(): pl.pallas_call(unsort, out_shape=jax.ShapeDtypeStruct((rows, out_cols), B...  3.03 us

profile of v2, /device:TPU:64, one launch (start us, length us, event | category | flops | bytes accessed | tf_op | source)
XLA Modules:
  0.0 112.7 jit_solution(3463528739319995118)
XLA Ops:
  0.0 109.5 %exchange.1 = (bf16[1024,512]{1,0:T(8,128)(2,1)}, s32[1,32]{1,0:T(1,128)}) custom-call(bf16[1024,256]{1,0:T(8,128)(2,1)} %q_hbm.1, bf16[400,256]{1,0:T(8,128)(2,1)} %bitcast.4, s32[1,32]{1,0:T(1,128)} %bitcast.6, s32[1,32]{1,0:T(1,128)} %bitcast.7, bf16[4096,512]{1,0:T(8,128)(2,1)} %w_hbm.1), custom_call_target="tpu_custom_call" | custom-call | tf_op jit(solution)/shard_map/exchange/pallas_call | solution.py:349
  109.5 3.0 %unsort.1 = bf16[1024,512]{1,0:T(8,128)(2,1)} custom-call(s32[32]{0:T(128)} %bitcast.5, bf16[1024,512]{1,0:T(8,128)(2,1)} %get-tuple-element.8.ordered), custom_call_target="tpu_custom_call" | custom-call | tf_op jit(solution)/shard_map/unsort/pallas_call | solution.py:383

commit v3 on v2

--- a/solution.py
+++ b/solution.py
@@ -11,6 +11,7 @@
 NEED = 4
 RING = 8
 SHARE = 4
+LANES = 8
 HEAD_DIM = 128
 MESH = pl.DeviceIdType.MESH
 F32 = jnp.float32
@@ -52,7 +53,7 @@
 def exchange(n_serve, chunks, q_hbm, kv_hbm, slot_ref, len_ref, w_hbm, out_hbm, place_out,
              qv, sq, vq, ao, kvb, g, wo, wp, acc, ps, pr, ob, live_ref,
              local_sem, ob_sem, kv_sr, kv_rr, kv_sl, kv_rl, q_s, q_r, ret_s, ret_r,
-             w_s, w_r, wf_s, wf_r, ag_sr, ag_rr, ag_sl, ag_rl, p_s, p_r):
+             w_s, w_r, ag_sr, ag_rr, ag_sl, ag_rl, p_s, p_r):
     s = lax.axis_index("serve")
     t = lax.axis_index("tensor")
     y = lax.rem(t, RING)
@@ -70,9 +71,15 @@
     slot_rows = rows // NEED
     piece = kv_hbm.shape[0]
     half, out_cols = wo.shape
-    wpart = half // 4
-
-    wait_entry = greet([owner[3], asker[3], owner[2], asker[2], owner[1], asker[1], mate, right, left])
+    wpart = half // LANES
+
+    lane = lax.rem(s, LANES)
+    x = lane // 2
+    x_up = (s - lane + lax.rem(lane + 2, LANES), t)
+    x_down = (s - lane + lax.rem(lane + LANES - 2, LANES), t)
+
+    wait_entry = greet([owner[3], asker[3], owner[2], asker[2], owner[1], asker[1],
+                        x_up, x_down, mate, right, left])
     q_load = pltpu.make_async_copy(q_hbm, qv, local_sem.at[0])
     q_load.start()
 
@@ -156,26 +163,51 @@
     def ask(c):
         return remote(part_of(sq, c), vq.at[spot(c), :], q_s.at[c], q_r.at[c], owner[chunks[c][2]])
 
-    def w_part(side, i):
-        return wp.at[pl.ds(pl.multiple_of(side * (2 * wpart) + i * wpart, wpart), wpart), :]
-
-    def w_out(i):
-        first = (1 - z) * half + core * (2 * wpart) + i * wpart
-        return remote(w_hbm.at[pl.ds(pl.multiple_of(first, wpart), wpart), :], w_part(core, i),
-                      w_s.at[i], w_r.at[i], mate)
-
-    def w_swap(i):
-        return remote(w_part(core, i), w_part(core, i), wf_s.at[i], wf_r.at[i], sibling)
-
-    def w_relay(i):
-        w_out(i).wait_recv()
-        w_swap(i).start()
+    def w_part(x_from, side, low=0, size=None):
+        first = (lax.rem(x_from + LANES, LANES // 2) * 2 + side) * wpart + low
+        return wp.at[pl.ds(pl.multiple_of(first, wpart // 2), size or wpart), :]
+
+    def w_send(i, x_from, side, device, low=0, size=None):
+        part = w_part(x_from, side, low, size)
+        return remote(part, part, w_s.at[i], w_r.at[i], device)
+
+    w_first = (1 - z) * half + lane * wpart
+    w_out = remote(w_hbm.at[pl.ds(pl.multiple_of(w_first, wpart), wpart), :], w_part(x, core),
+                   w_s.at[0], w_r.at[0], mate)
+    lower = wpart // 2
+    w_sends = [
+        w_out,
+        w_send(1, x, core, x_up), w_send(2, x, core, x_down), w_send(3, x, core, sibling),
+        w_send(4, x - 1, core, x_up, 0, lower), w_send(5, x - 1, core, sibling),
+        w_send(6, x + 1, core, x_down, lower, lower), w_send(7, x + 1, core, sibling),
+        w_send(8, x + 2, core, sibling, 0, lower), w_send(9, x + 2, core, sibling, lower, lower),
+    ]
+
+    def w_stage(i):
+        if i == 0:
+            w_out.wait_recv()
+            for n in (1, 2, 3):
+                w_sends[n].start()
+        elif i == 1:
+            w_send(1, x - 1, core, x_down).wait_recv()
+            w_sends[4].start()
+            w_sends[5].start()
+            w_send(2, x + 1, core, x_up).wait_recv()
+            w_sends[6].start()
+            w_sends[7].start()
+        else:
+            w_send(4, x + 2, core, x_down, 0, lower).wait_recv()
+            w_sends[8].start()
+            w_send(6, x + 2, core, x_up, lower, lower).wait_recv()
+            w_sends[9].start()
 
     def w_ready():
         w_load.wait()
-        for i in range(2):
-            part = w_part(1 - core, i)
-            remote(part, part, wf_s.at[i], wf_r.at[i], sibling).wait_recv()
+        w_send(3, x, 1 - core, sibling).wait_recv()
+        w_send(5, x - 1, 1 - core, sibling).wait_recv()
+        w_send(7, x + 1, 1 - core, sibling).wait_recv()
+        w_send(8, x + 2, 1 - core, sibling, 0, lower).wait_recv()
+        w_send(9, x + 2, 1 - core, sibling, lower, lower).wait_recv()
 
     count = len(chunks)
     visitors = [c for c in range(count) if chunks[c][2] > 0]
@@ -184,11 +216,11 @@
         for c in visitors:
             if chunks[c][2] == j:
                 ask(c).start()
-    w_out(0).start()
-    w_out(1).start()
+    w_out.start()
     kv_step(1)
     sort(0)
     kv_step(2)
+    w_stage(0)
     kv_step(3)
     kv_load.wait()
 
@@ -277,8 +309,8 @@
         tasks.append((ready[c] + 450 if c < count - 1 else 1e9, functools.partial(finish, c)))
     for i, c in enumerate(visitors):
         tasks.append((VISIT[chunks[c][2]] + i, functools.partial(visit, c)))
-    tasks.append((15, functools.partial(w_relay, 0)))
-    tasks.append((W_TIME, functools.partial(w_relay, 1)))
+    for i in (1, 2):
+        tasks.append((W_STAGE[i - 1], functools.partial(w_stage, i)))
     tasks.append((W_TIME + 1, w_ready))
     tasks.sort(key=lambda task: task[0])
     start(0)
@@ -297,9 +329,8 @@
     for c in visitors:
         ask(c).wait_send()
         answer(c).wait_send()
-    for i in range(2):
-        w_out(i).wait_send()
-        w_swap(i).wait_send()
+    for copy in w_sends:
+        copy.wait_send()
     for c in range(count):
         for k in range(reach_right[c]):
             go_right(c, k).wait_send()
@@ -309,8 +340,9 @@
         write(c).wait()
 
 
-LAG = 2.2
-W_TIME = 900
+LAG = 3.0
+W_TIME = 2000
+W_STAGE = [900, 1500]
 VISIT = [0, 10, 310, 620]
 
 
@@ -371,7 +403,7 @@
             dma((3,)), dma((count,)),
             dma((3,)), dma((3,)), dma((3,)), dma((3,)),
             dma((count,)), dma((count,)), dma((count,)), dma((count,)),
-            dma((2,)), dma((2,)), dma((2,)), dma((2,)),
+            dma((10,)), dma((10,)),
             dma((count, 4)), dma((count, 4)), dma((count, 4)), dma((count, 4)),
             dma((count,)), dma((count,)),
         ],

time: 113 us -> 101 us (0.89)
  the two profiles are of different devices: /device:TPU:64 before, /device:TPU:8 now
where the time goes in v3:
time: 101 us
  Pallas kernels  100 us (99%)
    pallas_call x1, Pallas kernels, on_device(): pl.pallas_call(functools.partial(exchange, lax.axis_size('serve'), chunks...  97.4 us
    pallas_call x1, Pallas kernels, on_device(): pl.pallas_call(unsort, out_shape=jax.ShapeDtypeStruct((rows, out_cols), B...  3.03 us

profile of v3, /device:TPU:8, one launch (start us, length us, event | category | flops | bytes accessed | tf_op | source)
XLA Modules:
  0.0 100.6 jit_solution(13255167527504617531)
XLA Ops:
  0.0 97.4 %exchange.1 = (bf16[1024,512]{1,0:T(8,128)(2,1)}, s32[1,32]{1,0:T(1,128)}) custom-call(bf16[1024,256]{1,0:T(8,128)(2,1)} %q_hbm.1, bf16[400,256]{1,0:T(8,128)(2,1)} %bitcast.4, s32[1,32]{1,0:T(1,128)} %bitcast.6, s32[1,32]{1,0:T(1,128)} %bitcast.7, bf16[4096,512]{1,0:T(8,128)(2,1)} %w_hbm.1), custom_call_target="tpu_custom_call" | custom-call | tf_op jit(solution)/shard_map/exchange/pallas_call | solution.py:381
  97.4 3.0 %unsort.1 = bf16[1024,512]{1,0:T(8,128)(2,1)} custom-call(s32[32]{0:T(128)} %bitcast.5, bf16[1024,512]{1,0:T(8,128)(2,1)} %get-tuple-element.8.ordered), custom_call_target="tpu_custom_call" | custom-call | tf_op jit(solution)/shard_map/unsort/pallas_call | solution.py:415

commit v4 on v3

--- a/solution.py
+++ b/solution.py
@@ -343,7 +343,7 @@
 LAG = 3.0
 W_TIME = 2000
 W_STAGE = [900, 1500]
-VISIT = [0, 10, 310, 620]
+VISIT = [0, 10, 650, 1300]
 
 
 def unsort(place_ref, ordered, out, held, in_sem, out_sem):

time: 101 us -> 99.3 us (0.983)
  Pallas kernels: 100 us -> 98.9 us
    pallas_call x1, Pallas kernels: 97.4 us -> 95.9 us  [on_device(): pl.pallas_call(functools.partial(exchange, lax.axis_size('serve'), chunks...]
where the time goes in v4:
time: 99.3 us; the launch traced here: 99.1 us
  Pallas kernels  98.9 us (100%)
    pallas_call x1, Pallas kernels, on_device(): pl.pallas_call(functools.partial(exchange, lax.axis_size('serve'), chunks...  95.9 us
    pallas_call x1, Pallas kernels, on_device(): pl.pallas_call(unsort, out_shape=jax.ShapeDtypeStruct((rows, out_cols), B...  3.03 us

profile of v4, /device:TPU:8, one launch (start us, length us, event | category | flops | bytes accessed | tf_op | source)
XLA Modules:
  0.0 99.1 jit_solution(5399866550349320777)
XLA Ops:
  0.0 95.9 %exchange.1 = (bf16[1024,512]{1,0:T(8,128)(2,1)}, s32[1,32]{1,0:T(1,128)}) custom-call(bf16[1024,256]{1,0:T(8,128)(2,1)} %q_hbm.1, bf16[400,256]{1,0:T(8,128)(2,1)} %bitcast.4, s32[1,32]{1,0:T(1,128)} %bitcast.6, s32[1,32]{1,0:T(1,128)} %bitcast.7, bf16[4096,512]{1,0:T(8,128)(2,1)} %w_hbm.1), custom_call_target="tpu_custom_call" | custom-call | tf_op jit(solution)/shard_map/exchange/pallas_call | solution.py:381
  95.9 3.0 %unsort.1 = bf16[1024,512]{1,0:T(8,128)(2,1)} custom-call(s32[32]{0:T(128)} %bitcast.5, bf16[1024,512]{1,0:T(8,128)(2,1)} %get-tuple-element.8.ordered), custom_call_target="tpu_custom_call" | custom-call | tf_op jit(solution)/shard_map/unsort/pallas_call | solution.py:415
